TPU v7x, 512 devices: a whole 4x8x8 slice. The times are simulated.
512 devices in a mesh: rad: 8 (over x, z_hi), ang: 32 (over z_lo, y), ax: 2 (over core).
Axes of the slice: x: 4, y: 8, z: 8 (z_hi: 2, z_lo: 4; z = z_hi * 4 + z_lo), core: 2. Of those that a mesh axis runs over, the one named last changes fastest.
Arguments:
- start_potential: float32 [128, 1536, 256], P('rad', 'ang', 'ax'), may hold values from -6 to 6
- charge_density: float32 [128, 1536, 256], P('rad', 'ang', 'ax'), may hold values from -12 to 12
- box_anchor: int32 [3, 2048], replicated, may hold values from 0 to 31, as said below
- box_extent: int32 [3, 2048], replicated, may hold values from 1 to 2, as said below
- atom_center: float32 [3, 2048], replicated, as said below
- atom_charge: float32 [2048], replicated, may hold values from 0.5 to 2
- atom_place: int32 [2048], replicated, may hold values from 0 to 2047, each once
Outputs:
- potential: float32 [128, 1536, 256], P('rad', 'ang', 'ax')
- forces: float32 [3, 2048], P(None, ('rad', 'ang', 'ax'))
Inputs may be any that keep to these rules, and one draw needn't show every extreme that they name: `box_anchor`: box anchors per dimension lie within that dimension's block count, the radial anchor plus extent never passes the last radial block, and at most 8 atoms share one anchor block. `box_extent`: at most 64 atom boxes cover any one block, and in every draw some block is covered by exactly 64. `atom_center`: each atom's center lies inside its box, in the box's unwrapped cell coordinates.
All inputs are finite; a program needn't handle non-finite values.
Results may differ from a plain program's by a relative error of at most 0.0003.
Values sent between devices are 32-bit elements; how exact they have to be, the bound alone decides.
A program may use at most 64 MiB of HBM per device.

v0:
```python
import math

import jax
import jax.numpy as jnp
from jax import lax
from jax.sharding import PartitionSpec as P

SWEEPS = 3
SLOTS = 64


cheb_low = 0.2
cheb_high = 2.0
highest = lax.Precision.HIGHEST


def with_halo(block, sides, width, periodic):
    for axis, dim in sides:
        count = lax.axis_size(axis)
        forward = [(i, i + 1) for i in range(count - 1)]
        if periodic:
            forward.append((count - 1, 0))
        backward = [(target, source) for source, target in forward]
        low = lax.ppermute(
            lax.slice_in_dim(block, block.shape[dim] - width, None, axis=dim), axis, forward
        )
        high = lax.ppermute(lax.slice_in_dim(block, 0, width, axis=dim), axis, backward)
        block = jnp.concatenate([low, block, high], axis=dim)
    return block


def sweep_weights(total_sweeps):
    middle = 0.5 * (cheb_high + cheb_low)
    spread = 0.5 * (cheb_high - cheb_low)
    return [
        1.0 / (middle + spread * math.cos(math.pi * (2 * number + 1) / (2 * total_sweeps)))
        for number in range(total_sweeps)
    ]


def relax_step(
    center,
    radial_up,
    radial_down,
    angle_next,
    angle_prev,
    axial_next,
    axial_prev,
    source,
    radius,
    angle_step,
    weight,
):
    lower_face = radius - 0.5
    upper_face = radius + 0.5
    angular = 1.0 / (radius * radius * (angle_step * angle_step))
    doubled = 2.0 * center
    applied = (upper_face * (center - radial_up) + lower_face * (center - radial_down)) / radius
    applied = (
        applied
        + angular * (doubled - angle_next - angle_prev)
        + (doubled - axial_next - axial_prev)
    )
    diagonal = (upper_face + lower_face) / radius + 2.0 * angular + 2.0
    return center + weight * (source - applied) / diagonal


def gaussian_pair(coords, middle_point, width):
    distance = coords - middle_point
    profile = jnp.exp(-(distance * distance) / (2.0 * width * width))
    return (profile, profile * (-distance / (width * width)))


def radius_rows(first_row, row_count, rad_total):
    row_index = first_row + jnp.arange(row_count, dtype=jnp.int32)
    radius = 0.5 * rad_total + row_index.astype(jnp.float32) + 0.5
    inside = (row_index >= 0) & (row_index < rad_total)
    return (radius[:, None, None], inside[:, None, None])


def shards(
    start_potential, charge_density, box_anchor, box_extent, atom_center, atom_charge, atom_place
):
    rad_cells, ang_cells, axial_cells = start_potential.shape
    rad_total = rad_cells * lax.axis_size("rad")
    angle_step = 2.0 * math.pi / (ang_cells * lax.axis_size("ang"))
    rad_start = lax.axis_index("rad") * rad_cells
    weights = sweep_weights(SWEEPS)
    radius, inside = radius_rows(rad_start, rad_cells, rad_total)
    potential = start_potential
    for sweep_index in range(SWEEPS):
        wrapped = with_halo(potential, (("ang", 1), ("ax", 2)), 1, True)
        layered = with_halo(potential, (("rad", 0),), 1, False)
        potential = relax_step(
            potential,
            layered[2:],
            layered[:-2],
            wrapped[:, 2:, 1:-1],
            wrapped[:, :-2, 1:-1],
            wrapped[:, 1:-1, 2:],
            wrapped[:, 1:-1, :-2],
            charge_density,
            radius,
            angle_step,
            weights[sweep_index],
        )
    width_rad = rad_cells / 3.0
    width_ang = ang_cells / 3.0
    width_axial = axial_cells / 3.0
    amplitude = 1.0 / math.sqrt(width_ang * width_axial / width_rad)
    offset_rad = lax.axis_index("rad") - box_anchor[0]
    offset_ang = jnp.remainder(lax.axis_index("ang") - box_anchor[1], lax.axis_size("ang"))
    offset_axial = jnp.remainder(lax.axis_index("ax") - box_anchor[2], lax.axis_size("ax"))
    covered = (
        (offset_rad >= 0)
        & (offset_rad < box_extent[0])
        & (offset_ang < box_extent[1])
        & (offset_axial < box_extent[2])
    )
    picked = jnp.nonzero(covered, size=SLOTS, fill_value=0)[0].astype(jnp.int32)
    occupied = jnp.arange(SLOTS, dtype=jnp.int32) < jnp.sum(covered.astype(jnp.int32))
    centers = atom_center[:, picked]
    coord_rad = (rad_start + jnp.arange(rad_cells, dtype=jnp.int32)).astype(jnp.float32)[:, None]
    rad_profile, rad_slope = gaussian_pair(coord_rad, centers[0][None, :], width_rad)
    start_ang = (box_anchor[1, picked] + offset_ang[picked]) * ang_cells
    coord_ang = (start_ang[None, :] + jnp.arange(ang_cells, dtype=jnp.int32)[:, None]).astype(
        jnp.float32
    )
    ang_profile, ang_slope = gaussian_pair(coord_ang, centers[1][None, :], width_ang)
    start_axial = (box_anchor[2, picked] + offset_axial[picked]) * axial_cells
    coord_axial = (start_axial[None, :] + jnp.arange(axial_cells, dtype=jnp.int32)[:, None]).astype(
        jnp.float32
    )
    axial_profile, axial_slope = gaussian_pair(coord_axial, centers[2][None, :], width_axial)
    axial_factors = jnp.concatenate([axial_profile, axial_slope], axis=1)
    projected = jnp.dot(
        potential.reshape(rad_cells * ang_cells, axial_cells),
        axial_factors,
        precision=highest,
        preferred_element_type=jnp.float32,
    )
    projected = projected.reshape(rad_cells, ang_cells, 2 * SLOTS)
    plain_part = projected[:, :, :SLOTS]
    sloped = projected[:, :, SLOTS:]
    along_r = jnp.einsum("ijs,js->is", plain_part, ang_profile, precision=highest)
    along_a = jnp.einsum("ijs,js->is", plain_part, ang_slope, precision=highest)
    along_z = jnp.einsum("ijs,js->is", sloped, ang_profile, precision=highest)
    radius_col = 0.5 * rad_total + coord_rad + 0.5
    weight_rad = angle_step * radius_col
    force_r = jnp.sum(weight_rad * rad_slope * along_r, axis=0)
    force_a = jnp.sum(rad_profile * along_a, axis=0)
    force_z = jnp.sum(weight_rad * rad_profile * along_z, axis=0)
    strength = jnp.where(occupied, atom_charge[picked] * amplitude, 0.0)
    pieces = jnp.stack([force_r, force_a, force_z]) * strength[None, :]
    places = atom_place[picked]
    onehot = (places[:, None] == jnp.arange(atom_place.shape[0], dtype=jnp.int32)[None, :]).astype(
        jnp.float32
    )
    partial_forces = jnp.dot(pieces, onehot, precision=highest, preferred_element_type=jnp.float32)
    forces = lax.psum_scatter(partial_forces, ("rad", "ang", "ax"), scatter_dimension=1, tiled=True)
    return (potential, forces)


def solution(mesh):
    placed = (P("rad", "ang", "ax"), P("rad", "ang", "ax"), P(), P(), P(), P(), P())
    return jax.shard_map(
        shards,
        mesh=mesh,
        in_specs=placed,
        out_specs=(P("rad", "ang", "ax"), P(None, ("rad", "ang", "ax"))),
        check_vma=False,
    )
```

profile of v0, /device:TPU:1, one launch (start us, length us, event | category | flops | bytes accessed | tf_op | source)
XLA Modules:
  0.0 215.0 jit_solution(4052317238193996186)
XLA Ops:
  1.5 11.4 %collective-permute-start.2 = (f32[16,1,128]{2,1,0:T(1,128)S(1)}, f32[16,1,128]{2,1,0:T(1,128)S(1)}, u32[]{:S(2)}, u32[]{:S(2)}) collective-permute-start(f32[16,1,128]{2,1,0:T(1,128)S(1)} %get-tuple-element.31), channel_id=1, source_target_pairs={{2,0},{4,2},{6,4},{8,6},{10,8},{12,10},{14,12},{16,14},{18,16},{20... | collective-permute-start | bytes 24584 | tf_op jit(solution)/shard_map/ppermute | solution.py:27
  12.9 1.9 collective-permute-start.3
  15.6 1.4 collective-permute-start
  17.0 8.6 %collective-permute-start.1 = (f32[1,48,128]{2,1,0:T(8,128)S(1)}, f32[1,48,128]{2,1,0:T(8,128)S(1)}, u32[]{:S(2)}, u32[]{:S(2)}) collective-permute-start(f32[1,48,128]{2,1,0:T(8,128)S(1)} %get-tuple-element.29), channel_id=1, source_target_pairs={{0,64},{64,128},{128,192},{192,256},{256,320},{320,384},{384,448},... | collective-permute-start | bytes 73736 | tf_op jit(solution)/shard_map/ppermute | solution.py:24
  26.4 14.7 %scatter_custom_fusion = s32[64]{0:T(128)S(1)} fusion(s32[2048]{0:T(1024)S(1)} %bitcast.57, s32[2048]{0:T(1024)S(1)} %rem.108, s32[]{:T(128)} %constant.122.clone.1), kind=kCustom, calls=%fused_computation.182 | custom fusion | flops 2048 | bytes 260 | tf_op jit(solution)/shard_map/scatter-add | solution.py:120
  42.7 0.9 gather_fusion.3
  49.1 3.1 %collective-permute-start.4 = (f32[16,50,1]{2,1,0:T(8,128)S(1)}, f32[16,50,1]{2,1,0:T(8,128)S(1)}, u32[]{:S(2)}, u32[]{:S(2)}) collective-permute-start(f32[16,50,1]{2,1,0:T(8,128)S(1)} %get-tuple-element.18), channel_id=1, source_target_pairs={{1,0},{0,1},{3,2},{2,3},{5,4},{4,5},{7,6},{6,7},{9,8},{8,9},{11,10... | collective-permute-start | bytes 9608 | tf_op jit(solution)/shard_map/ppermute | solution.py:27
  52.3 1.9 collective-permute-start.5
  54.2 1.8 collective-permute-done.5
  56.8 7.5 %collective-permute-start.8 = (f32[16,1,128]{2,1,0:T(1,128)S(1)}, f32[16,1,128]{2,1,0:T(1,128)S(1)}, u32[]{:S(2)}, u32[]{:S(2)}) collective-permute-start(f32[16,1,128]{2,1,0:T(1,128)S(1)} %get-tuple-element.27), channel_id=1, source_target_pairs={{2,0},{4,2},{6,4},{8,6},{10,8},{12,10},{14,12},{16,14},{18,16},{20... | collective-permute-start | bytes 24584 | tf_op jit(solution)/shard_map/ppermute | solution.py:27
  64.3 1.9 collective-permute-start.9
  66.3 1.3 collective-permute-start.6
  67.6 9.1 %collective-permute-start.7 = (f32[1,48,128]{2,1,0:T(8,128)S(1)}, f32[1,48,128]{2,1,0:T(8,128)S(1)}, u32[]{:S(2)}, u32[]{:S(2)}) collective-permute-start(f32[1,48,128]{2,1,0:T(8,128)S(1)} %get-tuple-element.25), channel_id=1, source_target_pairs={{0,64},{64,128},{128,192},{192,256},{256,320},{320,384},{384,448},... | collective-permute-start | bytes 73736 | tf_op jit(solution)/shard_map/ppermute | solution.py:24
  76.9 2.6 %collective-permute-start.10 = (f32[16,50,1]{2,1,0:T(8,128)S(1)}, f32[16,50,1]{2,1,0:T(8,128)S(1)}, u32[]{:S(2)}, u32[]{:S(2)}) collective-permute-start(f32[16,50,1]{2,1,0:T(8,128)S(1)} %get-tuple-element.16), channel_id=1, source_target_pairs={{1,0},{0,1},{3,2},{2,3},{5,4},{4,5},{7,6},{6,7},{9,8},{8,9},{11,10... | collective-permute-start | bytes 9608 | tf_op jit(solution)/shard_map/ppermute | solution.py:27
  79.6 1.9 collective-permute-start.11
  81.5 1.8 collective-permute-done.11
  84.1 7.5 %collective-permute-start.14 = (f32[16,1,128]{2,1,0:T(1,128)S(1)}, f32[16,1,128]{2,1,0:T(1,128)S(1)}, u32[]{:S(2)}, u32[]{:S(2)}) collective-permute-start(f32[16,1,128]{2,1,0:T(1,128)S(1)} %get-tuple-element.23), channel_id=1, source_target_pairs={{2,0},{4,2},{6,4},{8,6},{10,8},{12,10},{14,12},{16,14},{18,16},{20... | collective-permute-start | bytes 24584 | tf_op jit(solution)/shard_map/ppermute | solution.py:27
  91.6 1.9 collective-permute-start.15
  93.6 1.3 collective-permute-start.12
  94.9 9.1 %collective-permute-start.13 = (f32[1,48,128]{2,1,0:T(8,128)S(1)}, f32[1,48,128]{2,1,0:T(8,128)S(1)}, u32[]{:S(2)}, u32[]{:S(2)}) collective-permute-start(f32[1,48,128]{2,1,0:T(8,128)S(1)} %get-tuple-element.21), channel_id=1, source_target_pairs={{0,64},{64,128},{128,192},{192,256},{256,320},{320,384},{384,448},... | collective-permute-start | bytes 73736 | tf_op jit(solution)/shard_map/ppermute | solution.py:24
  104.2 2.6 %collective-permute-start.16 = (f32[16,50,1]{2,1,0:T(8,128)S(1)}, f32[16,50,1]{2,1,0:T(8,128)S(1)}, u32[]{:S(2)}, u32[]{:S(2)}) collective-permute-start(f32[16,50,1]{2,1,0:T(8,128)S(1)} %get-tuple-element.14), channel_id=1, source_target_pairs={{1,0},{0,1},{3,2},{2,3},{5,4},{4,5},{7,6},{6,7},{9,8},{8,9},{11,10... | collective-permute-start | bytes 9608 | tf_op jit(solution)/shard_map/ppermute | solution.py:27
  106.8 1.9 collective-permute-start.17
  109.6 1.0 collective-permute-done.17
  112.7 101.6 %all-reduce.2 = f32[3,2048]{1,0:T(4,128)S(1)} all-reduce(f32[3,2048]{1,0:T(4,128)S(1)} %fusion), channel_id=2, replica_groups=mesh['rad'=8,'ang'=32,'ax'=2] {'rad','ang','ax'}, use_global_device_ids=true, to_apply=%region_8.9.clone | all-reduce | flops 6144 | bytes 49152
  (85 shorter events, 15.0 us)
Async XLA Ops:
  0.6 46.6 %copy-start = (f32[2048]{0:T(1024)S(1)}, f32[2048]{0:T(1024)}, u32[]{:S(2)}) copy-start(f32[2048]{0:T(1024)} %param.12) | copy-start | bytes 24580
  1.5 47.3 %collective-permute-start.2 = (f32[16,1,128]{2,1,0:T(1,128)S(1)}, f32[16,1,128]{2,1,0:T(1,128)S(1)}, u32[]{:S(2)}, u32[]{:S(2)}) collective-permute-start(f32[16,1,128]{2,1,0:T(1,128)S(1)} %get-tuple-element.31), channel_id=1, source_target_pairs={{2,0},{4,2},{6,4},{8,6},{10,8},{12,10},{14,12},{16,14},{18,16},{20... | collective-permute-start | bytes 24584 | tf_op jit(solution)/shard_map/ppermute | solution.py:27
  12.9 36.0 %collective-permute-start.3 = (f32[16,1,128]{2,1,0:T(1,128)S(1)}, f32[16,1,128]{2,1,0:T(1,128)S(1)}, u32[]{:S(2)}, u32[]{:S(2)}) collective-permute-start(f32[16,1,128]{2,1,0:T(1,128)S(1)} %get-tuple-element.30), channel_id=1, source_target_pairs={{0,2},{2,4},{4,6},{6,8},{8,10},{10,12},{12,14},{14,16},{16,18},{18... | collective-permute-start | bytes 24584 | tf_op jit(solution)/shard_map/ppermute | solution.py:24
  14.8 10.8 %copy-start.7 = (s32[3,2048]{1,0:T(4,128)S(1)}, s32[3,2048]{1,0:T(4,128)}, u32[]{:S(2)}) copy-start(s32[3,2048]{1,0:T(4,128)} %param.10) | copy-start | bytes 73732
  15.6 10.1 %copy-start.1 = (s32[3,2048]{1,0:T(4,128)S(1)}, s32[3,2048]{1,0:T(4,128)}, u32[]{:S(2)}) copy-start(s32[3,2048]{1,0:T(4,128)} %param.9) | copy-start | bytes 73732
  15.6 40.4 %collective-permute-start = (f32[1,48,128]{2,1,0:T(8,128)S(1)}, f32[1,48,128]{2,1,0:T(8,128)S(1)}, u32[]{:S(2)}, u32[]{:S(2)}) collective-permute-start(f32[1,48,128]{2,1,0:T(8,128)S(1)} %get-tuple-element.28), channel_id=1, source_target_pairs={{64,0},{128,64},{192,128},{256,192},{320,256},{384,320},{448,384},... | collective-permute-start | bytes 73736 | tf_op jit(solution)/shard_map/ppermute | solution.py:27
  17.0 39.0 %collective-permute-start.1 = (f32[1,48,128]{2,1,0:T(8,128)S(1)}, f32[1,48,128]{2,1,0:T(8,128)S(1)}, u32[]{:S(2)}, u32[]{:S(2)}) collective-permute-start(f32[1,48,128]{2,1,0:T(8,128)S(1)} %get-tuple-element.29), channel_id=1, source_target_pairs={{0,64},{64,128},{128,192},{192,256},{256,320},{320,384},{384,448},... | collective-permute-start | bytes 73736 | tf_op jit(solution)/shard_map/ppermute | solution.py:24
  47.2 1.6 copy-start.4
  48.9 7.1 %copy-start.3 = (f32[16,48,128]{2,1,0:T(8,128)S(1)}, f32[16,48,128]{2,1,0:T(8,128)}, u32[]{:S(2)}) copy-start(f32[16,48,128]{2,1,0:T(8,128)} %param.8) | copy-start | bytes 1179652
  49.1 5.1 %collective-permute-start.4 = (f32[16,50,1]{2,1,0:T(8,128)S(1)}, f32[16,50,1]{2,1,0:T(8,128)S(1)}, u32[]{:S(2)}, u32[]{:S(2)}) collective-permute-start(f32[16,50,1]{2,1,0:T(8,128)S(1)} %get-tuple-element.18), channel_id=1, source_target_pairs={{1,0},{0,1},{3,2},{2,3},{5,4},{4,5},{7,6},{6,7},{9,8},{8,9},{11,10... | collective-permute-start | bytes 9608 | tf_op jit(solution)/shard_map/ppermute | solution.py:27
  52.3 3.7 %collective-permute-start.5 = (f32[16,50,1]{2,1,0:T(8,128)S(1)}, f32[16,50,1]{2,1,0:T(8,128)S(1)}, u32[]{:S(2)}, u32[]{:S(2)}) collective-permute-start(f32[16,50,1]{2,1,0:T(8,128)S(1)} %get-tuple-element.19), channel_id=1, source_target_pairs={{0,1},{1,0},{2,3},{3,2},{4,5},{5,4},{6,7},{7,6},{8,9},{9,8},{10,11... | collective-permute-start | bytes 9608 | tf_op jit(solution)/shard_map/ppermute | solution.py:24
  56.8 19.9 %collective-permute-start.8 = (f32[16,1,128]{2,1,0:T(1,128)S(1)}, f32[16,1,128]{2,1,0:T(1,128)S(1)}, u32[]{:S(2)}, u32[]{:S(2)}) collective-permute-start(f32[16,1,128]{2,1,0:T(1,128)S(1)} %get-tuple-element.27), channel_id=1, source_target_pairs={{2,0},{4,2},{6,4},{8,6},{10,8},{12,10},{14,12},{16,14},{18,16},{20... | collective-permute-start | bytes 24584 | tf_op jit(solution)/shard_map/ppermute | solution.py:27
  64.3 12.3 %collective-permute-start.9 = (f32[16,1,128]{2,1,0:T(1,128)S(1)}, f32[16,1,128]{2,1,0:T(1,128)S(1)}, u32[]{:S(2)}, u32[]{:S(2)}) collective-permute-start(f32[16,1,128]{2,1,0:T(1,128)S(1)} %get-tuple-element.26), channel_id=1, source_target_pairs={{0,2},{2,4},{4,6},{6,8},{8,10},{10,12},{12,14},{14,16},{16,18},{18... | collective-permute-start | bytes 24584 | tf_op jit(solution)/shard_map/ppermute | solution.py:24
  66.3 17.0 %collective-permute-start.6 = (f32[1,48,128]{2,1,0:T(8,128)S(1)}, f32[1,48,128]{2,1,0:T(8,128)S(1)}, u32[]{:S(2)}, u32[]{:S(2)}) collective-permute-start(f32[1,48,128]{2,1,0:T(8,128)S(1)} %get-tuple-element.24), channel_id=1, source_target_pairs={{64,0},{128,64},{192,128},{256,192},{320,256},{384,320},{448,384},... | collective-permute-start | bytes 73736 | tf_op jit(solution)/shard_map/ppermute | solution.py:27
  67.6 15.7 %collective-permute-start.7 = (f32[1,48,128]{2,1,0:T(8,128)S(1)}, f32[1,48,128]{2,1,0:T(8,128)S(1)}, u32[]{:S(2)}, u32[]{:S(2)}) collective-permute-start(f32[1,48,128]{2,1,0:T(8,128)S(1)} %get-tuple-element.25), channel_id=1, source_target_pairs={{0,64},{64,128},{128,192},{192,256},{256,320},{320,384},{384,448},... | collective-permute-start | bytes 73736 | tf_op jit(solution)/shard_map/ppermute | solution.py:24
  76.9 4.6 %collective-permute-start.10 = (f32[16,50,1]{2,1,0:T(8,128)S(1)}, f32[16,50,1]{2,1,0:T(8,128)S(1)}, u32[]{:S(2)}, u32[]{:S(2)}) collective-permute-start(f32[16,50,1]{2,1,0:T(8,128)S(1)} %get-tuple-element.16), channel_id=1, source_target_pairs={{1,0},{0,1},{3,2},{2,3},{5,4},{4,5},{7,6},{6,7},{9,8},{8,9},{11,10... | collective-permute-start | bytes 9608 | tf_op jit(solution)/shard_map/ppermute | solution.py:27
  79.6 3.7 %collective-permute-start.11 = (f32[16,50,1]{2,1,0:T(8,128)S(1)}, f32[16,50,1]{2,1,0:T(8,128)S(1)}, u32[]{:S(2)}, u32[]{:S(2)}) collective-permute-start(f32[16,50,1]{2,1,0:T(8,128)S(1)} %get-tuple-element.17), channel_id=1, source_target_pairs={{0,1},{1,0},{2,3},{3,2},{4,5},{5,4},{6,7},{7,6},{8,9},{9,8},{10,11... | collective-permute-start | bytes 9608 | tf_op jit(solution)/shard_map/ppermute | solution.py:24
  84.1 19.9 %collective-permute-start.14 = (f32[16,1,128]{2,1,0:T(1,128)S(1)}, f32[16,1,128]{2,1,0:T(1,128)S(1)}, u32[]{:S(2)}, u32[]{:S(2)}) collective-permute-start(f32[16,1,128]{2,1,0:T(1,128)S(1)} %get-tuple-element.23), channel_id=1, source_target_pairs={{2,0},{4,2},{6,4},{8,6},{10,8},{12,10},{14,12},{16,14},{18,16},{20... | collective-permute-start | bytes 24584 | tf_op jit(solution)/shard_map/ppermute | solution.py:27
  91.6 12.3 %collective-permute-start.15 = (f32[16,1,128]{2,1,0:T(1,128)S(1)}, f32[16,1,128]{2,1,0:T(1,128)S(1)}, u32[]{:S(2)}, u32[]{:S(2)}) collective-permute-start(f32[16,1,128]{2,1,0:T(1,128)S(1)} %get-tuple-element.22), channel_id=1, source_target_pairs={{0,2},{2,4},{4,6},{6,8},{8,10},{10,12},{12,14},{14,16},{16,18},{18... | collective-permute-start | bytes 24584 | tf_op jit(solution)/shard_map/ppermute | solution.py:24
  93.6 17.0 %collective-permute-start.12 = (f32[1,48,128]{2,1,0:T(8,128)S(1)}, f32[1,48,128]{2,1,0:T(8,128)S(1)}, u32[]{:S(2)}, u32[]{:S(2)}) collective-permute-start(f32[1,48,128]{2,1,0:T(8,128)S(1)} %get-tuple-element.20), channel_id=1, source_target_pairs={{64,0},{128,64},{192,128},{256,192},{320,256},{384,320},{448,384},... | collective-permute-start | bytes 73736 | tf_op jit(solution)/shard_map/ppermute | solution.py:27
  94.9 15.7 %collective-permute-start.13 = (f32[1,48,128]{2,1,0:T(8,128)S(1)}, f32[1,48,128]{2,1,0:T(8,128)S(1)}, u32[]{:S(2)}, u32[]{:S(2)}) collective-permute-start(f32[1,48,128]{2,1,0:T(8,128)S(1)} %get-tuple-element.21), channel_id=1, source_target_pairs={{0,64},{64,128},{128,192},{192,256},{256,320},{320,384},{384,448},... | collective-permute-start | bytes 73736 | tf_op jit(solution)/shard_map/ppermute | solution.py:24
  104.2 4.6 %copy-start.2 = (s32[2048]{0:T(1024)S(1)}, s32[2048]{0:T(1024)}, u32[]{:S(2)}) copy-start(s32[2048]{0:T(1024)} %param.13) | copy-start | bytes 24580
  104.2 5.4 %collective-permute-start.16 = (f32[16,50,1]{2,1,0:T(8,128)S(1)}, f32[16,50,1]{2,1,0:T(8,128)S(1)}, u32[]{:S(2)}, u32[]{:S(2)}) collective-permute-start(f32[16,50,1]{2,1,0:T(8,128)S(1)} %get-tuple-element.14), channel_id=1, source_target_pairs={{1,0},{0,1},{3,2},{2,3},{5,4},{4,5},{7,6},{6,7},{9,8},{8,9},{11,10... | collective-permute-start | bytes 9608 | tf_op jit(solution)/shard_map/ppermute | solution.py:27
  106.8 3.7 %collective-permute-start.17 = (f32[16,50,1]{2,1,0:T(8,128)S(1)}, f32[16,50,1]{2,1,0:T(8,128)S(1)}, u32[]{:S(2)}, u32[]{:S(2)}) collective-permute-start(f32[16,50,1]{2,1,0:T(8,128)S(1)} %get-tuple-element.15), channel_id=1, source_target_pairs={{0,1},{1,0},{2,3},{3,2},{4,5},{5,4},{6,7},{7,6},{8,9},{9,8},{10,11... | collective-permute-start | bytes 9608 | tf_op jit(solution)/shard_map/ppermute | solution.py:24
  (2 other events, 1.7 us)
where the time goes:
time: 216 us; the launch traced here: 215 us
  blocking collectives  102 us (47%)
  starting transfers between devices  77.1 us (36%)
  other arithmetic  20.2 us (9%)
  local copies, waits for them, and re-layouts  9.57 us (4%)
  waiting for transfers between devices  4.53 us (2%)
    unnamed x1, blocking collectives  102 us
    ppermute x9, starting transfers between devices, with_halo(): lax.ppermute(lax.slice_in_dim(block, 0, width, axis=dim), axis, backward)  38.8 us
    ppermute x9, starting transfers between devices, with_halo(): lax.ppermute(lax.slice_in_dim(block, block.shape[dim] - width, None, axis...  38.2 us
    scatter-add x1, other arithmetic, shards(): picked = jnp.nonzero(covered, size=SLOTS, fill_value=0)[0].astype(jnp.int32)  14.7 us
    ppermute x9, waiting for transfers between devices, with_halo(): lax.ppermute(lax.slice_in_dim(block, block.shape[dim] - width, None, axis...  4.51 us
  transfers between devices with their start and end apart: 18, of which 3 were waited for; matrix products, arithmetic and copies ran while one was open for 12% of the time, Pallas kernels for 0%

commit v1 on v0

v1 whole, which is shorter than its diff:
```python
import functools
import math

import jax
import jax.numpy as jnp
from jax import lax
from jax.experimental import pallas as pl
from jax.experimental.pallas import tpu as pltpu
from jax.sharding import PartitionSpec as P

SWEEPS = 3
GHOST = 3
CR, CA, CZ = 16, 48, 128
N_RAD, N_ANG, N_AX = 8, 32, 2
ROWS = CA + 8
PLANES = CR + 2 * GHOST
SLOTS = 256
ATOMS = 2048
MESH = pl.DeviceIdType.MESH
F32, BF16 = jnp.float32, jnp.bfloat16

cheb_low = 0.2
cheb_high = 2.0


def sweep_weights(total_sweeps):
    middle = 0.5 * (cheb_high + cheb_low)
    spread = 0.5 * (cheb_high - cheb_low)
    return [
        1.0 / (middle + spread * math.cos(math.pi * (2 * number + 1) / (2 * total_sweeps)))
        for number in range(total_sweeps)
    ]


def far_first(count):
    return sorted(range(1, count), key=lambda d: -min(d, count - d))


def plane_peers(r, a, x):
    me_x, z_hi, z_lo, me_y = r // 2, lax.rem(r, 2), a // 8, lax.rem(a, 8)
    order = [(dx, dy) for dx in range(4) for dy in range(8) if dx or dy]
    order.sort(key=lambda d: -(min(d[0], 4 - d[0]) + min(d[1], 8 - d[1])))
    for dx, dy in order:
        tx, ty = lax.rem(me_x + dx, 4), lax.rem(me_y + dy, 8)
        yield dx * 8 + dy, (tx * 2 + z_hi, z_lo * 8 + ty, x), tx * 8 + ty


def column_peers(r, a, x):
    me_x, me_y = r // 2, lax.rem(a, 8)
    me = (lax.rem(r, 2) * 4 + a // 8) * 2 + x
    for d in far_first(16):
        t = lax.rem(me + d, 16)
        tz = t // 2
        yield d, (me_x * 2 + tz // 4, lax.rem(tz, 4) * 8 + me_y, lax.rem(t, 2))


def split2(value):
    high = value.astype(BF16)
    return high, (value - high.astype(F32)).astype(BF16)


def split3(value):
    parts = []
    for _ in range(3):
        part = value.astype(BF16).astype(F32)
        parts.append(part)
        value = value - part
    return parts


def shape_pair(distance, valid, width):
    profile = jnp.where(valid, jnp.exp(-(distance * distance) / (2.0 * width * width)), 0.0)
    return profile, profile * (-distance / (width * width))


def iota(shape, dim):
    return lax.broadcasted_iota(jnp.int32, shape, dim)


def nt(left, right):
    return lax.dot_general(left, right, (((1,), (1,)), ((), ())), preferred_element_type=F32)


def slot_table(r, a, x, anchor_ref, extent_ref, center_ref, charge_ref, place_ref):
    anchor = [anchor_ref[d : d + 1, :] for d in range(3)]
    extent = [extent_ref[d : d + 1, :] for d in range(3)]
    back_r = r - anchor[0]
    back_a = (a - anchor[1]) & (N_ANG - 1)
    back_x = (x - anchor[2]) & (N_AX - 1)
    near = (
        (back_r >= -1) & (back_r <= extent[0]) & (((back_a + 1) & (N_ANG - 1)) <= extent[1] + 1)
    )
    mask = jnp.where(near, 1.0, 0.0)
    chunks = ATOMS // 128
    rows = jnp.concatenate([mask[:, 128 * k : 128 * (k + 1)] for k in range(chunks)], axis=0)
    rows16 = rows.astype(BF16)
    before = jnp.where(iota((128, 128), 0) < iota((128, 128), 1), 1.0, 0.0).astype(BF16)
    above = jnp.where(iota((chunks, chunks), 1) < iota((chunks, chunks), 0), 1.0, 0.0).astype(BF16)
    rank = jnp.dot(rows16, before, preferred_element_type=F32)
    rank = rank + jnp.sum(jnp.dot(above, rows16, preferred_element_type=F32), axis=1, keepdims=True)
    rank = jnp.where(rows > 0.5, rank, -1.0)
    slot = iota((SLOTS, 128), 0).astype(F32)
    pick = jnp.concatenate(
        [
            jnp.where(jnp.broadcast_to(rank[k : k + 1, :], (SLOTS, 128)) == slot, 1.0, 0.0).astype(BF16)
            for k in range(chunks)
        ],
        axis=1,
    )
    data = []
    for d, cells in enumerate((CR, CA, CZ)):
        data += split3(center_ref[d : d + 1, :] - (anchor[d] * cells).astype(F32))
    data += split3(charge_ref[...])
    place = place_ref[...]
    data += [v.astype(F32) for v in (back_r, back_a, back_x, *extent)]
    data.append((((place >> 9) * 8) + ((place >> 3) & 7)).astype(F32))
    data.append(
        (((place >> 8) & 1) * 32 + ((place >> 6) & 3) * 8 + (place & 7)).astype(F32)
    )
    data += [jnp.zeros((1, ATOMS), F32)] * 4
    table = nt(pick, jnp.concatenate(data, axis=0).astype(BF16))
    return table.T


def kernel(
    start_ref,
    source_ref,
    anchor_ref,
    extent_ref,
    center_ref,
    charge_ref,
    place_ref,
    out_ref,
    force_ref,
    va,
    vax,
    vb,
    vbx,
    src,
    coef,
    shape_r,
    ax_in,
    full,
    edge,
    rad_in,
    ang_in,
    corner_in,
    part,
    plane_in,
    mine,
    column_in,
    sems,
):
    r, a, x = lax.axis_index("rad"), lax.axis_index("ang"), lax.axis_index("ax")
    up, down = lax.rem(r + 1, N_RAD), lax.rem(r + N_RAD - 1, N_RAD)
    nxt, prv = lax.rem(a + 1, N_ANG), lax.rem(a + N_ANG - 1, N_ANG)
    plane = list(plane_peers(r, a, x))
    column = list(column_peers(r, a, x))
    around = [(up, a, x), (down, a, x), (r, nxt, x), (r, prv, x)]
    around += [(up, nxt, x), (down, nxt, x), (up, prv, x), (down, prv, x)]

    barrier = pltpu.get_barrier_semaphore()
    targets = [p[1] for p in plane] + [p[1] for p in column] + around
    for target in targets:
        pl.semaphore_signal(barrier, inc=1, device_id=target, device_id_type=MESH)

    for ref in (va, vax, vb, vbx, src):
        ref[...] = jnp.zeros_like(ref)
    va[4 : 4 + CR, 0:CA, :] = start_ref[...]
    src[4 : 4 + CR, 0:CA, :] = source_ref[...]

    step = 2.0 * math.pi / (CA * N_ANG)
    index = r * CR + iota((24, CZ), 0) - 4
    radius = 0.5 * (CR * N_RAD) + index.astype(F32) + 0.5
    inside = (index >= 0) & (index < CR * N_RAD)
    upper, lower = (radius + 0.5) / radius, (radius - 0.5) / radius
    angular = 1.0 / (radius * radius * (step * step))
    inverse = jnp.where(inside, 1.0 / (upper + lower + 2.0 * angular + 2.0), 0.0)
    coef[0] = inverse
    coef[1] = inverse * upper
    coef[2] = inverse * lower
    coef[3] = inverse * angular

    lane = iota((ROWS, CZ), 1)
    first, last = lane == 0, lane == CZ - 1
    buffers = [(va, vax), (vb, vbx)]
    for number, weight in enumerate(sweep_weights(SWEEPS)):
        (own, other), (own_new, other_new) = buffers[number % 2], buffers[1 - number % 2]

        def sweep(p, carry, own=own, other=other, own_new=own_new, other_new=other_new, weight=weight):
            c = [jnp.broadcast_to(coef[k, pl.ds(p, 1), :], (ROWS, CZ)) for k in range(4)]
            v, w = own[p], other[p]
            v_next, v_prev = pltpu.roll(v, CZ - 1, 1), pltpu.roll(v, 1, 1)
            w_next, w_prev = pltpu.roll(w, CZ - 1, 1), pltpu.roll(w, 1, 1)
            for here, there, centre, axial, extra in (
                (own, own_new, v, (jnp.where(last, w_next, v_next), jnp.where(first, w_prev, v_prev)), src),
                (other, other_new, w, (jnp.where(last, v_next, w_next), jnp.where(first, v_prev, w_prev)), None),
            ):
                along = axial[0] + axial[1]
                if extra is not None:
                    along = along + extra[p]
                turn = pltpu.roll(centre, ROWS - 1, 0) + pltpu.roll(centre, 1, 0)
                applied = c[0] * along + c[1] * here[p + 1] + c[2] * here[p - 1] + c[3] * turn
                there[p] = centre + weight * (applied - centre)
            return carry

        reach = number + 1
        lax.fori_loop(4 - reach, 4 + CR + reach, sweep, 0)
    own, other = buffers[SWEEPS % 2]

    table = slot_table(r, a, x, anchor_ref, extent_ref, center_ref, charge_ref, place_ref)

    def entry(k):
        return table[k : k + 1, :]

    centre = [entry(3 * d) + entry(3 * d + 1) + entry(3 * d + 2) for d in range(3)]
    charge = entry(9) + entry(10) + entry(11)
    back, span = [entry(12 + d) for d in range(3)], [entry(15 + d) for d in range(3)]
    width = (CR / 3.0, CA / 3.0, CZ / 3.0)
    amplitude = 1.0 / math.sqrt(width[1] * width[2] / width[0])

    cell = iota((24, SLOTS), 0).astype(F32) - GHOST
    d = cell + back[0] * CR
    profile, slope = shape_pair(d - centre[0], (d >= 0.0) & (d < span[0] * CR), width[0])
    arc = step * (0.5 * (CR * N_RAD) + (r * CR).astype(F32) + cell + 0.5)
    shape_r[0] = arc * slope
    shape_r[1] = profile
    shape_r[2] = arc * profile

    row = iota((ROWS, SLOTS), 0)
    d = jnp.where(row >= CA + 4, row - ROWS, row).astype(F32) + back[1] * CA
    d = jnp.where(d < 0.0, d + CA * N_ANG, d)
    d = jnp.where(d >= CA * N_ANG, d - CA * N_ANG, d)
    ang_profile, ang_slope = shape_pair(d - centre[1], d < span[1] * CA, width[1])

    d = iota((2 * CZ, SLOTS), 0).astype(F32) + back[2] * CZ
    d = jnp.where(d >= CZ * N_AX, d - CZ * N_AX, d)
    ax_profile, ax_slope = shape_pair(d - centre[2], d < span[2] * CZ, width[2])
    ax_high, ax_low = split2(jnp.concatenate([ax_profile, ax_slope], axis=1))

    per = PLANES // 2

    def project(part_index, sums):
        first_plane = part_index * per
        block = jnp.concatenate(
            [
                own[pl.ds(1 + first_plane, per)].reshape(per * ROWS, CZ),
                other[pl.ds(1 + first_plane, per)].reshape(per * ROWS, CZ),
            ],
            axis=1,
        )
        high, low = split2(block)
        projected = jnp.dot(high, ax_high, preferred_element_type=F32)
        projected = projected + jnp.dot(high, ax_low, preferred_element_type=F32)
        projected = projected + jnp.dot(low, ax_high, preferred_element_type=F32)
        sums = list(sums)
        for p in range(per):
            along = [jnp.zeros((8, SLOTS), F32)] * 3
            for t in range(ROWS // 8):
                top = p * ROWS + 8 * t
                plain, sloped = projected[top : top + 8, :SLOTS], projected[top : top + 8, SLOTS:]
                ang_p, ang_s = ang_profile[8 * t : 8 * t + 8], ang_slope[8 * t : 8 * t + 8]
                along = [along[0] + plain * ang_p, along[1] + plain * ang_s, along[2] + sloped * ang_p]
            for k in range(3):
                sums[k] = sums[k] + shape_r[k, pl.ds(first_plane + p, 1), :] * along[k]
        return tuple(sums)

    sums = lax.fori_loop(0, 2, project, tuple(jnp.zeros((8, SLOTS), F32) for _ in range(3)))
    strength = charge * amplitude
    force = [jnp.sum(s, axis=0, keepdims=True) * strength for s in sums]

    target, low = entry(18), entry(19)
    to = jnp.where(iota((32, SLOTS), 0).astype(F32) == target, 1.0, 0.0).astype(BF16)
    here = iota((64, SLOTS), 0).astype(F32) == low
    spread = jnp.concatenate([jnp.where(here, f, 0.0) for f in force] + [jnp.zeros((64, SLOTS), F32)], axis=0)
    placed = jnp.zeros((32, 256), F32)
    for piece in split3(spread):
        placed = placed + nt(to, piece.astype(BF16))
    for k in range(32):
        part[k] = placed[k : k + 1, :]

    pl.semaphore_wait(barrier, len(targets))

    def send(source, landing, number, device):
        copy = pltpu.make_async_remote_copy(
            src_ref=source,
            dst_ref=landing,
            send_sem=sems.at[0, number],
            recv_sem=sems.at[1, number],
            device_id=device,
            device_id_type=MESH,
        )
        copy.start()
        return copy

    def wait(ref, side, number):
        pltpu.make_async_copy(ref, ref, sems.at[side, number]).wait()

    ax_copy = send(other.at[pl.ds(1, PLANES)], ax_in, 0, (r, a, 1 - x))
    for slot, device, place in plane:
        send(part.at[place], plane_in.at[slot - 1], 1, device)

    ax_copy.wait()
    for p in range(PLANES):
        value = own[1 + p] + ax_in[p]
        full[p] = value[0:CA]
        edge[0, p] = value[CA : CA + 4]
        edge[1, p] = value[CA + 4 :]
    lo, hi = pl.ds(0, GHOST), pl.ds(PLANES - GHOST, GHOST)
    copies = [
        send(full.at[hi], rad_in.at[0], 2, around[0]),
        send(full.at[lo], rad_in.at[1], 3, around[1]),
        send(edge.at[0, pl.ds(GHOST, CR)], ang_in.at[0], 4, around[2]),
        send(edge.at[1, pl.ds(GHOST, CR)], ang_in.at[1], 5, around[3]),
        send(edge.at[0, hi], corner_in.at[0], 6, around[4]),
        send(edge.at[0, lo], corner_in.at[1], 7, around[5]),
        send(edge.at[1, hi], corner_in.at[2], 8, around[6]),
        send(edge.at[1, lo], corner_in.at[3], 9, around[7]),
    ]
    out_ref[...] = full[pl.ds(GHOST, CR)]

    wait(plane_in, 1, 1)
    me_place = (r // 2) * 8 + lax.rem(a, 8)
    mine[...] = part[me_place] + jnp.sum(plane_in[...], axis=0)
    for slot, device in column:
        send(mine, column_in.at[slot - 1], 10, device)

    for copy in copies[2:]:
        copy.wait()
    out_ref[:, 0:4, :] = out_ref[:, 0:4, :] + ang_in[0]
    out_ref[:, CA - 4 : CA, :] = out_ref[:, CA - 4 : CA, :] + ang_in[1]
    for k, (planes, rows) in enumerate(
        ((slice(0, 3), slice(0, 4)), (slice(13, 16), slice(0, 4)), (slice(0, 3), slice(44, 48)), (slice(13, 16), slice(44, 48)))
    ):
        out_ref[planes, rows, :] = out_ref[planes, rows, :] + corner_in[k]
    for copy in copies[:2]:
        copy.wait()
    out_ref[0:3] = out_ref[0:3] + rad_in[0]
    out_ref[13:16] = out_ref[13:16] + rad_in[1]

    wait(column_in, 1, 10)
    total = mine[...] + jnp.sum(column_in[...], axis=0)
    me_column = (lax.rem(r, 2) * 4 + a // 8) * 2 + x
    for k in range(3):
        turned = pltpu.roll(jnp.broadcast_to(total, (8, 256)), lax.rem(512 - 64 * k - 4 * me_column, 256), 1)
        force_ref[k : k + 1, :] = turned[0:1, 0:4]
    wait(plane_in, 0, 1)
    wait(column_in, 0, 10)


def shards(start_potential, charge_density, box_anchor, box_extent, atom_center, atom_charge, atom_place):
    whole = pl.BlockSpec(memory_space=pltpu.VMEM)
    grid = (PLANES + 2, ROWS, CZ)
    return pl.pallas_call(
        kernel,
        out_shape=(
            jax.ShapeDtypeStruct((CR, CA, CZ), F32),
            jax.ShapeDtypeStruct((3, 4), F32),
        ),
        in_specs=[whole] * 7,
        out_specs=(whole, whole),
        scratch_shapes=[
            *[pltpu.VMEM(grid, F32)] * 5,
            pltpu.VMEM((4, 24, CZ), F32),
            pltpu.VMEM((3, 24, SLOTS), F32),
            pltpu.VMEM((PLANES, ROWS, CZ), F32),
            pltpu.VMEM((PLANES, CA, CZ), F32),
            pltpu.VMEM((2, PLANES, 4, CZ), F32),
            pltpu.VMEM((2, GHOST, CA, CZ), F32),
            pltpu.VMEM((2, CR, 4, CZ), F32),
            pltpu.VMEM((4, GHOST, 4, CZ), F32),
            pltpu.VMEM((32, 1, 256), F32),
            pltpu.VMEM((31, 1, 256), F32),
            pltpu.VMEM((1, 256), F32),
            pltpu.VMEM((15, 1, 256), F32),
            pltpu.SemaphoreType.DMA((2, 11)),
        ],
        compiler_params=pltpu.CompilerParams(
            collective_id=0, has_side_effects=True, vmem_limit_bytes=40 * 1024 * 1024
        ),
    )(
        start_potential,
        charge_density,
        box_anchor,
        box_extent,
        atom_center,
        atom_charge.reshape(1, ATOMS),
        atom_place.reshape(1, ATOMS),
    )


def solution(mesh):
    placed = (P("rad", "ang", "ax"), P("rad", "ang", "ax"), P(), P(), P(), P(), P())
    return jax.shard_map(
        shards,
        mesh=mesh,
        in_specs=placed,
        out_specs=(P("rad", "ang", "ax"), P(None, ("rad", "ang", "ax"))),
        check_vma=False,
    )
```

time: 216 us -> 41.1 us (0.19)
  blocking collectives: 102 us -> 0 us
  starting transfers between devices: 77.1 us -> 0 us
  Pallas kernels: 0 us -> 33 us
  other arithmetic: 20.2 us -> 0 us
  waiting for transfers between devices: 4.53 us -> 0 us
  local copies, waits for them, and re-layouts: 9.57 us -> 6.97 us
    unnamed x1 -> x0, blocking collectives: 102 us -> none
    ppermute x18 -> x0, starting transfers between devices: 77.1 us -> none  [the longest x9 38.8 us: with_halo(): lax.ppermute(lax.slice_in_dim(block, 0, width, axis=dim), axis, backward)]
    pallas_call x0 -> x1, Pallas kernels: none -> 33 us  [shards(): pl.pallas_call(kernel, out_shape=(jax.ShapeDtypeStruct((CR, CA, CZ), F32)...]
    scatter-add x1 -> x0, other arithmetic: 14.7 us -> none  [shards(): picked = jnp.nonzero(covered, size=SLOTS, fill_value=0)[0].astype(jnp.int32)]
    unnamed x18 -> x16, local copies, waits for them, and re-layouts: 1.31 us -> 6.97 us
    gather x7 -> x0, local copies, waits for them, and re-layouts: 5.52 us -> none  [the longest x2 1.69 us: shards(): start_axial = (box_anchor[2, picked] + offset_axial[picked]) * axial_cells]
    ppermute x18 -> x0, waiting for transfers between devices: 4.53 us -> none  [the longest x9 4.51 us: with_halo(): lax.ppermute(lax.slice_in_dim(block, block.shape[dim] - width, None, axis...]
    slice x12 -> x0, local copies, waits for them, and re-layouts: 2.53 us -> none  [the longest x6 1.34 us: with_halo(): lax.slice_in_dim(block, 0, width, axis=dim)]
  transfers between devices with their start and end apart: 18 -> 0, of which waited for: 3 -> 0; matrix products, arithmetic and copies ran while one was open for 12% -> 0% of each run, Pallas kernels for 0% -> 0%
where the time goes in v1:
time: 41.1 us; the launch traced here: 40.6 us
  Pallas kernels  33 us (80%)
  local copies, waits for them, and re-layouts  6.97 us (17%)
  between operations  0.66 us (2%)
    pallas_call x1, Pallas kernels, shards(): pl.pallas_call(kernel, out_shape=(jax.ShapeDtypeStruct((CR, CA, CZ), F32)...  33 us
    unnamed x16, local copies, waits for them, and re-layouts  6.97 us

profile of v1, /device:TPU:1, one launch (start us, length us, event | category | flops | bytes accessed | tf_op | source)
XLA Modules:
  0.0 40.6 jit_solution(1624756322298458229)
XLA Ops:
  0.6 0.0 copy-start
  0.6 1.0 %copy-done = f32[16,48,128]{2,1,0:T(8,128)S(1)} copy-done((f32[16,48,128]{2,1,0:T(8,128)S(1)}, f32[16,48,128]{2,1,0:T(8,128)}, u32[]{:S(2)}) %copy-start) | copy-done | bytes 393240
  1.6 0.0 copy-start.1
  1.6 1.0 %copy-done.1 = f32[16,48,128]{2,1,0:T(8,128)S(1)} copy-done((f32[16,48,128]{2,1,0:T(8,128)S(1)}, f32[16,48,128]{2,1,0:T(8,128)}, u32[]{:S(2)}) %copy-start.1) | copy-done | bytes 393240
  2.6 0.0 copy-start.2
  2.6 0.8 %copy-done.2 = s32[3,2048]{1,0:T(4,128)S(1)} copy-done((s32[3,2048]{1,0:T(4,128)S(1)}, s32[3,2048]{1,0:T(4,128)}, u32[]{:S(2)}) %copy-start.2) | copy-done | bytes 24600
  3.4 0.0 copy-start.3
  3.4 0.8 %copy-done.3 = s32[3,2048]{1,0:T(4,128)S(1)} copy-done((s32[3,2048]{1,0:T(4,128)S(1)}, s32[3,2048]{1,0:T(4,128)}, u32[]{:S(2)}) %copy-start.3) | copy-done | bytes 24600
  4.1 0.0 copy-start.4
  4.1 0.8 %copy-done.4 = f32[3,2048]{1,0:T(4,128)S(1)} copy-done((f32[3,2048]{1,0:T(4,128)S(1)}, f32[3,2048]{1,0:T(4,128)}, u32[]{:S(2)}) %copy-start.4) | copy-done | bytes 24600
  4.9 0.0 copy-start.5
  4.9 0.7 %copy-done.5 = f32[2048]{0:T(1024)S(1)} copy-done((f32[2048]{0:T(1024)S(1)}, f32[2048]{0:T(1024)}, u32[]{:S(2)}) %copy-start.5) | copy-done | bytes 8216
  5.6 0.0 copy-start.6
  5.6 0.7 %copy-done.6 = s32[2048]{0:T(1024)S(1)} copy-done((s32[2048]{0:T(1024)S(1)}, s32[2048]{0:T(1024)}, u32[]{:S(2)}) %copy-start.6) | copy-done | bytes 8216
  6.3 33.0 %shard_map.86 = (f32[16,48,128]{2,1,0:T(8,128)S(1)}, f32[3,4]{1,0:T(4,128)S(1)}) custom-call(f32[16,48,128]{2,1,0:T(8,128)S(1)} %copy-done, f32[16,48,128]{2,1,0:T(8,128)S(1)} %copy-done.1, s32[3,2048]{1,0:T(4,128)S(1)} %copy-done.2, s32[3,2048]{1,0:T(4,128)S(1)} %copy-done.3, f32[3,2048]{1,0:T(4,128)S(1)} %copy-done.4, f32[1,2048]{1,0:T(1,128)S(1)} %bitcast.2, ...), custom_call_target="tpu_custom_call" | custom-call | tf_op jit(solution)/shard_map/pallas_call | solution.py:354
  39.3 0.7 %copy.11 = f32[16,48,128]{2,1,0:T(8,128)} copy(f32[16,48,128]{2,1,0:T(8,128)S(1)} %get-tuple-element.4) | data formatting | bytes 786432
  40.0 0.6 %copy.12 = f32[3,4]{1,0:T(4,128)} copy(f32[3,4]{1,0:T(4,128)S(1)} %get-tuple-element.5) | data formatting | bytes 96
Async XLA Ops:
  0.6 1.0 %copy-start = (f32[16,48,128]{2,1,0:T(8,128)S(1)}, f32[16,48,128]{2,1,0:T(8,128)}, u32[]{:S(2)}) copy-start(f32[16,48,128]{2,1,0:T(8,128)} %start_ref.1) | copy-start | bytes 1179652
  1.6 1.0 %copy-start.1 = (f32[16,48,128]{2,1,0:T(8,128)S(1)}, f32[16,48,128]{2,1,0:T(8,128)}, u32[]{:S(2)}) copy-start(f32[16,48,128]{2,1,0:T(8,128)} %source_ref.1) | copy-start | bytes 1179652
  2.6 0.8 %copy-start.2 = (s32[3,2048]{1,0:T(4,128)S(1)}, s32[3,2048]{1,0:T(4,128)}, u32[]{:S(2)}) copy-start(s32[3,2048]{1,0:T(4,128)} %anchor_ref.1) | copy-start | bytes 73732
  3.4 0.8 %copy-start.3 = (s32[3,2048]{1,0:T(4,128)S(1)}, s32[3,2048]{1,0:T(4,128)}, u32[]{:S(2)}) copy-start(s32[3,2048]{1,0:T(4,128)} %extent_ref.1) | copy-start | bytes 73732
  4.1 0.8 %copy-start.4 = (f32[3,2048]{1,0:T(4,128)S(1)}, f32[3,2048]{1,0:T(4,128)}, u32[]{:S(2)}) copy-start(f32[3,2048]{1,0:T(4,128)} %center_ref.1) | copy-start | bytes 73732
  4.9 0.7 %copy-start.5 = (f32[2048]{0:T(1024)S(1)}, f32[2048]{0:T(1024)}, u32[]{:S(2)}) copy-start(f32[2048]{0:T(1024)} %param.12) | copy-start | bytes 24580
  5.6 0.7 %copy-start.6 = (s32[2048]{0:T(1024)S(1)}, s32[2048]{0:T(1024)}, u32[]{:S(2)}) copy-start(s32[2048]{0:T(1024)} %param.13) | copy-start | bytes 24580

commit v2 on v1

--- a/solution.py
+++ b/solution.py
@@ -123,13 +123,13 @@
 
 
 def kernel(
-    start_ref,
-    source_ref,
-    anchor_ref,
-    extent_ref,
-    center_ref,
-    charge_ref,
-    place_ref,
+    start_hbm,
+    source_hbm,
+    anchor_hbm,
+    extent_hbm,
+    center_hbm,
+    charge_hbm,
+    place_hbm,
     out_ref,
     force_ref,
     va,
@@ -149,8 +149,28 @@
     plane_in,
     mine,
     column_in,
+    anchor_ref,
+    extent_ref,
+    center_ref,
+    charge_ref,
+    place_ref,
     sems,
+    in_sems,
 ):
+    cells = (pl.ds(4, CR), pl.ds(0, CA))
+    fetch = [
+        (start_hbm, va.at[cells]),
+        (source_hbm, src.at[cells]),
+        (anchor_hbm, anchor_ref),
+        (extent_hbm, extent_ref),
+        (center_hbm, center_ref),
+        (charge_hbm, charge_ref),
+        (place_hbm, place_ref),
+    ]
+    fetch = [pltpu.make_async_copy(*pair, in_sems.at[k]) for k, pair in enumerate(fetch)]
+    for copy in fetch:
+        copy.start()
+
     r, a, x = lax.axis_index("rad"), lax.axis_index("ang"), lax.axis_index("ax")
     up, down = lax.rem(r + 1, N_RAD), lax.rem(r + N_RAD - 1, N_RAD)
     nxt, prv = lax.rem(a + 1, N_ANG), lax.rem(a + N_ANG - 1, N_ANG)
@@ -164,10 +184,16 @@
     for target in targets:
         pl.semaphore_signal(barrier, inc=1, device_id=target, device_id_type=MESH)
 
-    for ref in (va, vax, vb, vbx, src):
-        ref[...] = jnp.zeros_like(ref)
-    va[4 : 4 + CR, 0:CA, :] = start_ref[...]
-    src[4 : 4 + CR, 0:CA, :] = source_ref[...]
+    va[4 : 4 + CR, CA:, :] = jnp.zeros((CR, ROWS - CA, CZ), F32)
+    src[4 : 4 + CR, CA:, :] = jnp.zeros((CR, ROWS - CA, CZ), F32)
+    empty = jnp.zeros((ROWS, CZ), F32)
+    for p in (0, 1, 2, 3, 20, 21, 22, 23):
+        va[p] = empty
+    for p in (0, 1, 22, 23):
+        vax[p] = empty
+    for p in (1, 2, 21, 22):
+        vb[p] = empty
+        vbx[p] = empty
 
     step = 2.0 * math.pi / (CA * N_ANG)
     index = r * CR + iota((24, CZ), 0) - 4
@@ -181,31 +207,35 @@
     coef[2] = inverse * lower
     coef[3] = inverse * angular
 
+    for copy in fetch:
+        copy.wait()
+
     lane = iota((ROWS, CZ), 1)
     first, last = lane == 0, lane == CZ - 1
     buffers = [(va, vax), (vb, vbx)]
     for number, weight in enumerate(sweep_weights(SWEEPS)):
         (own, other), (own_new, other_new) = buffers[number % 2], buffers[1 - number % 2]
-
-        def sweep(p, carry, own=own, other=other, own_new=own_new, other_new=other_new, weight=weight):
-            c = [jnp.broadcast_to(coef[k, pl.ds(p, 1), :], (ROWS, CZ)) for k in range(4)]
-            v, w = own[p], other[p]
+        for p in range(3 - number, 5 + CR + number):
+            c = [jnp.broadcast_to(coef[k, p : p + 1, :], (ROWS, CZ)) for k in range(4)]
+            v = own[p]
             v_next, v_prev = pltpu.roll(v, CZ - 1, 1), pltpu.roll(v, 1, 1)
-            w_next, w_prev = pltpu.roll(w, CZ - 1, 1), pltpu.roll(w, 1, 1)
-            for here, there, centre, axial, extra in (
-                (own, own_new, v, (jnp.where(last, w_next, v_next), jnp.where(first, w_prev, v_prev)), src),
-                (other, other_new, w, (jnp.where(last, v_next, w_next), jnp.where(first, v_prev, w_prev)), None),
-            ):
-                along = axial[0] + axial[1]
-                if extra is not None:
-                    along = along + extra[p]
-                turn = pltpu.roll(centre, ROWS - 1, 0) + pltpu.roll(centre, 1, 0)
-                applied = c[0] * along + c[1] * here[p + 1] + c[2] * here[p - 1] + c[3] * turn
-                there[p] = centre + weight * (applied - centre)
-            return carry
-
-        reach = number + 1
-        lax.fori_loop(4 - reach, 4 + CR + reach, sweep, 0)
+            if number == 0:
+                along = jnp.where(last, 0.0, v_next) + jnp.where(first, 0.0, v_prev)
+                across = jnp.where(last, v_next, 0.0) + jnp.where(first, v_prev, 0.0)
+                other_new[p] = weight * (c[0] * across)
+            else:
+                w = other[p]
+                w_next, w_prev = pltpu.roll(w, CZ - 1, 1), pltpu.roll(w, 1, 1)
+                along = jnp.where(last, w_next, v_next) + jnp.where(first, w_prev, v_prev)
+                across = jnp.where(last, v_next, w_next) + jnp.where(first, v_prev, w_prev)
+                turn = pltpu.roll(w, ROWS - 1, 0) + pltpu.roll(w, 1, 0)
+                applied = c[0] * across + c[1] * other[p + 1] + c[2] * other[p - 1] + c[3] * turn
+                other_new[p] = w + weight * (applied - w)
+            if 4 <= p < 4 + CR:
+                along = along + src[p]
+            turn = pltpu.roll(v, ROWS - 1, 0) + pltpu.roll(v, 1, 0)
+            applied = c[0] * along + c[1] * own[p + 1] + c[2] * own[p - 1] + c[3] * turn
+            own_new[p] = v + weight * (applied - v)
     own, other = buffers[SWEEPS % 2]
 
     table = slot_table(r, a, x, anchor_ref, extent_ref, center_ref, charge_ref, place_ref)
@@ -350,6 +380,8 @@
 
 def shards(start_potential, charge_density, box_anchor, box_extent, atom_center, atom_charge, atom_place):
     whole = pl.BlockSpec(memory_space=pltpu.VMEM)
+    operands = [start_potential, charge_density, box_anchor, box_extent, atom_center]
+    operands += [atom_charge.reshape(1, ATOMS), atom_place.reshape(1, ATOMS)]
     grid = (PLANES + 2, ROWS, CZ)
     return pl.pallas_call(
         kernel,
@@ -357,7 +389,7 @@
             jax.ShapeDtypeStruct((CR, CA, CZ), F32),
             jax.ShapeDtypeStruct((3, 4), F32),
         ),
-        in_specs=[whole] * 7,
+        in_specs=[pl.BlockSpec(memory_space=pltpu.HBM)] * 7,
         out_specs=(whole, whole),
         scratch_shapes=[
             *[pltpu.VMEM(grid, F32)] * 5,
@@ -373,20 +405,18 @@
             pltpu.VMEM((31, 1, 256), F32),
             pltpu.VMEM((1, 256), F32),
             pltpu.VMEM((15, 1, 256), F32),
+            pltpu.VMEM((3, ATOMS), jnp.int32),
+            pltpu.VMEM((3, ATOMS), jnp.int32),
+            pltpu.VMEM((3, ATOMS), F32),
+            pltpu.VMEM((1, ATOMS), F32),
+            pltpu.VMEM((1, ATOMS), jnp.int32),
             pltpu.SemaphoreType.DMA((2, 11)),
+            pltpu.SemaphoreType.DMA((7,)),
         ],
         compiler_params=pltpu.CompilerParams(
             collective_id=0, has_side_effects=True, vmem_limit_bytes=40 * 1024 * 1024
         ),
-    )(
-        start_potential,
-        charge_density,
-        box_anchor,
-        box_extent,
-        atom_center,
-        atom_charge.reshape(1, ATOMS),
-        atom_place.reshape(1, ATOMS),
-    )
+    )(*[pltpu.with_memory_space_constraint(v, pltpu.HBM) for v in operands])
 
 
 def solution(mesh):

time: 41.1 us -> 32.8 us (0.80)
  local copies, waits for them, and re-layouts: 6.97 us -> 1.33 us
  Pallas kernels: 33 us -> 30.7 us
    unnamed x16 -> x2, local copies, waits for them, and re-layouts: 6.97 us -> 1.33 us
    pallas_call x1, Pallas kernels: 33 us -> 30.7 us  [shards(): pl.pallas_call(kernel, out_shape=(jax.ShapeDtypeStruct((CR, CA, CZ), F32)...]
where the time goes in v2:
time: 32.8 us; the launch traced here: 32.7 us
  Pallas kernels  30.7 us (94%)
  local copies, waits for them, and re-layouts  1.33 us (4%)
  between operations  0.64 us (2%)
    pallas_call x1, Pallas kernels, shards(): pl.pallas_call(kernel, out_shape=(jax.ShapeDtypeStruct((CR, CA, CZ), F32)...  30.7 us
    unnamed x2, local copies, waits for them, and re-layouts  1.33 us

profile of v2, /device:TPU:1, one launch (start us, length us, event | category | flops | bytes accessed | tf_op | source)
XLA Modules:
  0.0 32.7 jit_solution(13761834311240364851)
XLA Ops:
  0.6 30.7 %shard_map.86 = (f32[16,48,128]{2,1,0:T(8,128)S(1)}, f32[3,4]{1,0:T(4,128)S(1)}) custom-call(f32[16,48,128]{2,1,0:T(8,128)} %start_hbm.1, f32[16,48,128]{2,1,0:T(8,128)} %source_hbm.1, s32[3,2048]{1,0:T(4,128)} %anchor_hbm.1, s32[3,2048]{1,0:T(4,128)} %extent_hbm.1, f32[3,2048]{1,0:T(4,128)} %center_hbm.1, f32[1,2048]{1,0:T(1,128)} %bitcast.2, s32[1,2048]{1,0:T(1,128)} %bitcast.3), custom_call_target="tpu_custom_call" | custom-call | tf_op jit(solution)/shard_map/pallas_call | solution.py:386
  31.4 0.7 %copy.11 = f32[16,48,128]{2,1,0:T(8,128)} copy(f32[16,48,128]{2,1,0:T(8,128)S(1)} %get-tuple-element.4) | data formatting | bytes 786432
  32.1 0.6 %copy.12 = f32[3,4]{1,0:T(4,128)} copy(f32[3,4]{1,0:T(4,128)S(1)} %get-tuple-element.5) | data formatting | bytes 96

commit v3 on v2

--- a/solution.py
+++ b/solution.py
@@ -326,28 +326,46 @@
     def wait(ref, side, number):
         pltpu.make_async_copy(ref, ref, sems.at[side, number]).wait()
 
-    ax_copy = send(other.at[pl.ds(1, PLANES)], ax_in, 0, (r, a, 1 - x))
     for slot, device, place in plane:
         send(part.at[place], plane_in.at[slot - 1], 1, device)
-
-    ax_copy.wait()
-    for p in range(PLANES):
-        value = own[1 + p] + ax_in[p]
+    rows = pl.ds(0, CA)
+    far = [
+        send(own.at[22, rows], rad_in.at[0, 2], 2, around[0]),
+        send(own.at[1, rows], rad_in.at[1, 0], 3, around[1]),
+    ]
+    partner = (r, a, 1 - x)
+    below, above, inner = pl.ds(2, 2), pl.ds(20, 2), pl.ds(4, CR)
+    ax_copies = [
+        send(other.at[planes], ax_in.at[planes], number, partner)
+        for planes, number in ((above, 0), (below, 11), (inner, 12))
+    ]
+
+    def join(p):
+        value = own[p] + ax_in[p]
         full[p] = value[0:CA]
         edge[0, p] = value[CA : CA + 4]
         edge[1, p] = value[CA + 4 :]
-    lo, hi = pl.ds(0, GHOST), pl.ds(PLANES - GHOST, GHOST)
+
+    ax_copies[0].wait_recv()
+    join(20)
+    join(21)
+    near = [send(full.at[above], rad_in.at[0, pl.ds(0, 2)], 13, around[0])]
+    ax_copies[1].wait_recv()
+    join(2)
+    join(3)
+    near.append(send(full.at[below], rad_in.at[1, pl.ds(1, 2)], 14, around[1]))
     copies = [
-        send(full.at[hi], rad_in.at[0], 2, around[0]),
-        send(full.at[lo], rad_in.at[1], 3, around[1]),
-        send(edge.at[0, pl.ds(GHOST, CR)], ang_in.at[0], 4, around[2]),
-        send(edge.at[1, pl.ds(GHOST, CR)], ang_in.at[1], 5, around[3]),
-        send(edge.at[0, hi], corner_in.at[0], 6, around[4]),
-        send(edge.at[0, lo], corner_in.at[1], 7, around[5]),
-        send(edge.at[1, hi], corner_in.at[2], 8, around[6]),
-        send(edge.at[1, lo], corner_in.at[3], 9, around[7]),
-    ]
-    out_ref[...] = full[pl.ds(GHOST, CR)]
+        send(edge.at[0, above], corner_in.at[0], 6, around[4]),
+        send(edge.at[0, below], corner_in.at[1], 7, around[5]),
+        send(edge.at[1, above], corner_in.at[2], 8, around[6]),
+        send(edge.at[1, below], corner_in.at[3], 9, around[7]),
+    ]
+    ax_copies[2].wait_recv()
+    for p in range(4, 4 + CR):
+        join(p)
+    copies.append(send(edge.at[0, inner], ang_in.at[0], 4, around[2]))
+    copies.append(send(edge.at[1, inner], ang_in.at[1], 5, around[3]))
+    out_ref[...] = full[inner]
 
     wait(plane_in, 1, 1)
     me_place = (r // 2) * 8 + lax.rem(a, 8)
@@ -355,18 +373,20 @@
     for slot, device in column:
         send(mine, column_in.at[slot - 1], 10, device)
 
-    for copy in copies[2:]:
+    for copy in copies:
         copy.wait()
     out_ref[:, 0:4, :] = out_ref[:, 0:4, :] + ang_in[0]
     out_ref[:, CA - 4 : CA, :] = out_ref[:, CA - 4 : CA, :] + ang_in[1]
-    for k, (planes, rows) in enumerate(
-        ((slice(0, 3), slice(0, 4)), (slice(13, 16), slice(0, 4)), (slice(0, 3), slice(44, 48)), (slice(13, 16), slice(44, 48)))
-    ):
+    for k in range(4):
+        planes = pl.ds(14 * (k % 2), 2)
+        rows = pl.ds((CA - 4) * (k // 2), 4)
         out_ref[planes, rows, :] = out_ref[planes, rows, :] + corner_in[k]
-    for copy in copies[:2]:
+    for copy in far + near:
         copy.wait()
     out_ref[0:3] = out_ref[0:3] + rad_in[0]
     out_ref[13:16] = out_ref[13:16] + rad_in[1]
+    for copy in ax_copies:
+        copy.wait_send()
 
     wait(column_in, 1, 10)
     total = mine[...] + jnp.sum(column_in[...], axis=0)
@@ -378,12 +398,23 @@
     wait(column_in, 0, 10)
 
 
+def store(potential_ref, force_ref, potential_out, force_out, sems):
+    copies = [
+        pltpu.make_async_copy(potential_ref, potential_out, sems.at[0]),
+        pltpu.make_async_copy(force_ref, force_out, sems.at[1]),
+    ]
+    for copy in copies:
+        copy.start()
+    for copy in copies:
+        copy.wait()
+
+
 def shards(start_potential, charge_density, box_anchor, box_extent, atom_center, atom_charge, atom_place):
     whole = pl.BlockSpec(memory_space=pltpu.VMEM)
     operands = [start_potential, charge_density, box_anchor, box_extent, atom_center]
     operands += [atom_charge.reshape(1, ATOMS), atom_place.reshape(1, ATOMS)]
     grid = (PLANES + 2, ROWS, CZ)
-    return pl.pallas_call(
+    potential, forces = pl.pallas_call(
         kernel,
         out_shape=(
             jax.ShapeDtypeStruct((CR, CA, CZ), F32),
@@ -395,12 +426,12 @@
             *[pltpu.VMEM(grid, F32)] * 5,
             pltpu.VMEM((4, 24, CZ), F32),
             pltpu.VMEM((3, 24, SLOTS), F32),
-            pltpu.VMEM((PLANES, ROWS, CZ), F32),
-            pltpu.VMEM((PLANES, CA, CZ), F32),
-            pltpu.VMEM((2, PLANES, 4, CZ), F32),
+            pltpu.VMEM(grid, F32),
+            pltpu.VMEM((PLANES + 2, CA, CZ), F32),
+            pltpu.VMEM((2, PLANES + 2, 4, CZ), F32),
             pltpu.VMEM((2, GHOST, CA, CZ), F32),
             pltpu.VMEM((2, CR, 4, CZ), F32),
-            pltpu.VMEM((4, GHOST, 4, CZ), F32),
+            pltpu.VMEM((4, 2, 4, CZ), F32),
             pltpu.VMEM((32, 1, 256), F32),
             pltpu.VMEM((31, 1, 256), F32),
             pltpu.VMEM((1, 256), F32),
@@ -410,13 +441,24 @@
             pltpu.VMEM((3, ATOMS), F32),
             pltpu.VMEM((1, ATOMS), F32),
             pltpu.VMEM((1, ATOMS), jnp.int32),
-            pltpu.SemaphoreType.DMA((2, 11)),
+            pltpu.SemaphoreType.DMA((2, 15)),
             pltpu.SemaphoreType.DMA((7,)),
         ],
         compiler_params=pltpu.CompilerParams(
             collective_id=0, has_side_effects=True, vmem_limit_bytes=40 * 1024 * 1024
         ),
     )(*[pltpu.with_memory_space_constraint(v, pltpu.HBM) for v in operands])
+    hbm = pl.BlockSpec(memory_space=pltpu.HBM)
+    return pl.pallas_call(
+        store,
+        out_shape=(
+            jax.ShapeDtypeStruct((CR, CA, CZ), F32),
+            jax.ShapeDtypeStruct((3, 4), F32),
+        ),
+        in_specs=[whole] * 2,
+        out_specs=(hbm, hbm),
+        scratch_shapes=[pltpu.SemaphoreType.DMA((2,))],
+    )(*[pltpu.with_memory_space_constraint(v, pltpu.VMEM) for v in (potential, forces)])
 
 
 def solution(mesh):

time: 32.8 us -> 30.1 us (0.918)
  Pallas kernels: 30.7 us -> 29.3 us
  local copies, waits for them, and re-layouts: 1.33 us -> 0 us
    pallas_call x1, Pallas kernels: 30.7 us -> 28.6 us  [shards(): pl.pallas_call(kernel, out_shape=(jax.ShapeDtypeStruct((CR, CA, CZ), F32)...]
    unnamed x2 -> x0, local copies, waits for them, and re-layouts: 1.33 us -> none
    pallas_call x0 -> x1, Pallas kernels: none -> 0.77 us  [shards(): pl.pallas_call(store, out_shape=(jax.ShapeDtypeStruct((CR, CA, CZ), F32),...]
where the time goes in v3:
time: 30.1 us; the launch traced here: 30 us
  Pallas kernels  29.3 us (97%)
  between operations  0.64 us (2%)
    pallas_call x1, Pallas kernels, shards(): pl.pallas_call(kernel, out_shape=(jax.ShapeDtypeStruct((CR, CA, CZ), F32)...  28.6 us
    pallas_call x1, Pallas kernels, shards(): pl.pallas_call(store, out_shape=(jax.ShapeDtypeStruct((CR, CA, CZ), F32),...  0.77 us

profile of v3, /device:TPU:1, one launch (start us, length us, event | category | flops | bytes accessed | tf_op | source)
XLA Modules:
  0.0 30.0 jit_solution(2097870555596649905)
XLA Ops:
  0.6 28.6 %shard_map.86 = (f32[16,48,128]{2,1,0:T(8,128)S(1)}, f32[3,4]{1,0:T(4,128)S(1)}) custom-call(f32[16,48,128]{2,1,0:T(8,128)} %start_hbm.1, f32[16,48,128]{2,1,0:T(8,128)} %source_hbm.1, s32[3,2048]{1,0:T(4,128)} %anchor_hbm.1, s32[3,2048]{1,0:T(4,128)} %extent_hbm.1, f32[3,2048]{1,0:T(4,128)} %center_hbm.1, f32[1,2048]{1,0:T(1,128)} %bitcast.2, s32[1,2048]{1,0:T(1,128)} %bitcast.3), custom_call_target="tpu_custom_call" | custom-call | tf_op jit(solution)/shard_map/pallas_call | solution.py:417
  29.2 0.8 %shard_map.87 = (f32[16,48,128]{2,1,0:T(8,128)}, f32[3,4]{1,0:T(4,128)}) custom-call(f32[16,48,128]{2,1,0:T(8,128)S(1)} %get-tuple-element.4.potential_ref, f32[3,4]{1,0:T(4,128)S(1)} %get-tuple-element.5.force_ref), custom_call_target="tpu_custom_call" | custom-call | tf_op jit(solution)/shard_map/pallas_call | solution.py:452

commit v4 on v3

--- a/solution.py
+++ b/solution.py
@@ -13,6 +13,7 @@
 CR, CA, CZ = 16, 48, 128
 N_RAD, N_ANG, N_AX = 8, 32, 2
 ROWS = CA + 8
+FIRST = 4
 PLANES = CR + 2 * GHOST
 SLOTS = 256
 ATOMS = 2048
@@ -157,7 +158,21 @@
     sems,
     in_sems,
 ):
-    cells = (pl.ds(4, CR), pl.ds(0, CA))
+    r, a, x = lax.axis_index("rad"), lax.axis_index("ang"), lax.axis_index("ax")
+    up, down = lax.rem(r + 1, N_RAD), lax.rem(r + N_RAD - 1, N_RAD)
+    nxt, prv = lax.rem(a + 1, N_ANG), lax.rem(a + N_ANG - 1, N_ANG)
+    plane = list(plane_peers(r, a, x))
+    column = list(column_peers(r, a, x))
+    around = [(up, a, x), (down, a, x), (r, nxt, x), (r, prv, x)]
+    around += [(up, nxt, x), (down, nxt, x), (up, prv, x), (down, prv, x)]
+
+    barrier = pltpu.get_barrier_semaphore()
+    targets = around + [p[1] for p in column] + [p[1] for p in plane]
+    for target in targets:
+        pl.semaphore_signal(barrier, inc=1, device_id=target, device_id_type=MESH)
+
+    cells = (pl.ds(4, CR), pl.ds(8, CA))
+    window = pl.ds(FIRST, ROWS)
     fetch = [
         (start_hbm, va.at[cells]),
         (source_hbm, src.at[cells]),
@@ -171,29 +186,18 @@
     for copy in fetch:
         copy.start()
 
-    r, a, x = lax.axis_index("rad"), lax.axis_index("ang"), lax.axis_index("ax")
-    up, down = lax.rem(r + 1, N_RAD), lax.rem(r + N_RAD - 1, N_RAD)
-    nxt, prv = lax.rem(a + 1, N_ANG), lax.rem(a + N_ANG - 1, N_ANG)
-    plane = list(plane_peers(r, a, x))
-    column = list(column_peers(r, a, x))
-    around = [(up, a, x), (down, a, x), (r, nxt, x), (r, prv, x)]
-    around += [(up, nxt, x), (down, nxt, x), (up, prv, x), (down, prv, x)]
-
-    barrier = pltpu.get_barrier_semaphore()
-    targets = [p[1] for p in plane] + [p[1] for p in column] + around
-    for target in targets:
-        pl.semaphore_signal(barrier, inc=1, device_id=target, device_id_type=MESH)
-
-    va[4 : 4 + CR, CA:, :] = jnp.zeros((CR, ROWS - CA, CZ), F32)
-    src[4 : 4 + CR, CA:, :] = jnp.zeros((CR, ROWS - CA, CZ), F32)
-    empty = jnp.zeros((ROWS, CZ), F32)
+    strip = jnp.zeros((PLANES + 2, 8, CZ), F32)
+    for ref in (va, vax, vb, vbx, src):
+        ref[:, 0:8, :] = strip
+        ref[:, 56:64, :] = strip
+    empty = jnp.zeros((CA, CZ), F32)
     for p in (0, 1, 2, 3, 20, 21, 22, 23):
-        va[p] = empty
+        va[p, 8:56] = empty
     for p in (0, 1, 22, 23):
-        vax[p] = empty
+        vax[p, 8:56] = empty
     for p in (1, 2, 21, 22):
-        vb[p] = empty
-        vbx[p] = empty
+        vb[p, 8:56] = empty
+        vbx[p, 8:56] = empty
 
     step = 2.0 * math.pi / (CA * N_ANG)
     index = r * CR + iota((24, CZ), 0) - 4
@@ -216,26 +220,26 @@
     for number, weight in enumerate(sweep_weights(SWEEPS)):
         (own, other), (own_new, other_new) = buffers[number % 2], buffers[1 - number % 2]
         for p in range(3 - number, 5 + CR + number):
-            c = [jnp.broadcast_to(coef[k, p : p + 1, :], (ROWS, CZ)) for k in range(4)]
-            v = own[p]
+            c = [jnp.broadcast_to(weight * coef[k, p : p + 1, :], (ROWS, CZ)) for k in range(4)]
+            v = own[p, window]
             v_next, v_prev = pltpu.roll(v, CZ - 1, 1), pltpu.roll(v, 1, 1)
             if number == 0:
                 along = jnp.where(last, 0.0, v_next) + jnp.where(first, 0.0, v_prev)
                 across = jnp.where(last, v_next, 0.0) + jnp.where(first, v_prev, 0.0)
-                other_new[p] = weight * (c[0] * across)
+                other_new[p, window] = c[0] * across
             else:
-                w = other[p]
+                w = other[p, window]
                 w_next, w_prev = pltpu.roll(w, CZ - 1, 1), pltpu.roll(w, 1, 1)
                 along = jnp.where(last, w_next, v_next) + jnp.where(first, w_prev, v_prev)
                 across = jnp.where(last, v_next, w_next) + jnp.where(first, v_prev, w_prev)
-                turn = pltpu.roll(w, ROWS - 1, 0) + pltpu.roll(w, 1, 0)
-                applied = c[0] * across + c[1] * other[p + 1] + c[2] * other[p - 1] + c[3] * turn
-                other_new[p] = w + weight * (applied - w)
+                turn = other[p, pl.ds(FIRST + 1, ROWS)] + other[p, pl.ds(FIRST - 1, ROWS)]
+                applied = c[0] * across + c[1] * other[p + 1, window] + c[2] * other[p - 1, window] + c[3] * turn
+                other_new[p, window] = (1.0 - weight) * w + applied
             if 4 <= p < 4 + CR:
-                along = along + src[p]
-            turn = pltpu.roll(v, ROWS - 1, 0) + pltpu.roll(v, 1, 0)
-            applied = c[0] * along + c[1] * own[p + 1] + c[2] * own[p - 1] + c[3] * turn
-            own_new[p] = v + weight * (applied - v)
+                along = along + src[p, window]
+            turn = own[p, pl.ds(FIRST + 1, ROWS)] + own[p, pl.ds(FIRST - 1, ROWS)]
+            applied = c[0] * along + c[1] * own[p + 1, window] + c[2] * own[p - 1, window] + c[3] * turn
+            own_new[p, window] = (1.0 - weight) * v + applied
     own, other = buffers[SWEEPS % 2]
 
     table = slot_table(r, a, x, anchor_ref, extent_ref, center_ref, charge_ref, place_ref)
@@ -257,8 +261,7 @@
     shape_r[1] = profile
     shape_r[2] = arc * profile
 
-    row = iota((ROWS, SLOTS), 0)
-    d = jnp.where(row >= CA + 4, row - ROWS, row).astype(F32) + back[1] * CA
+    d = iota((ROWS, SLOTS), 0).astype(F32) - FIRST + back[1] * CA
     d = jnp.where(d < 0.0, d + CA * N_ANG, d)
     d = jnp.where(d >= CA * N_ANG, d - CA * N_ANG, d)
     ang_profile, ang_slope = shape_pair(d - centre[1], d < span[1] * CA, width[1])
@@ -267,23 +270,20 @@
     d = jnp.where(d >= CZ * N_AX, d - CZ * N_AX, d)
     ax_profile, ax_slope = shape_pair(d - centre[2], d < span[2] * CZ, width[2])
     ax_high, ax_low = split2(jnp.concatenate([ax_profile, ax_slope], axis=1))
-
-    per = PLANES // 2
-
-    def project(part_index, sums):
-        first_plane = part_index * per
+    ax_factors = jnp.concatenate([ax_high, ax_high, ax_low], axis=0)
+
+
+    sums = [jnp.zeros((8, SLOTS), F32) for _ in range(3)]
+
+    def project(first_plane, per):
         block = jnp.concatenate(
-            [
-                own[pl.ds(1 + first_plane, per)].reshape(per * ROWS, CZ),
-                other[pl.ds(1 + first_plane, per)].reshape(per * ROWS, CZ),
-            ],
+            [ref[pl.ds(1 + first_plane, per), window].reshape(per * ROWS, CZ) for ref in (own, other)],
             axis=1,
         )
         high, low = split2(block)
-        projected = jnp.dot(high, ax_high, preferred_element_type=F32)
-        projected = projected + jnp.dot(high, ax_low, preferred_element_type=F32)
-        projected = projected + jnp.dot(low, ax_high, preferred_element_type=F32)
-        sums = list(sums)
+        projected = jnp.dot(
+            jnp.concatenate([high, low, high], axis=1), ax_factors, preferred_element_type=F32
+        )
         for p in range(per):
             along = [jnp.zeros((8, SLOTS), F32)] * 3
             for t in range(ROWS // 8):
@@ -292,10 +292,12 @@
                 ang_p, ang_s = ang_profile[8 * t : 8 * t + 8], ang_slope[8 * t : 8 * t + 8]
                 along = [along[0] + plain * ang_p, along[1] + plain * ang_s, along[2] + sloped * ang_p]
             for k in range(3):
-                sums[k] = sums[k] + shape_r[k, pl.ds(first_plane + p, 1), :] * along[k]
-        return tuple(sums)
-
-    sums = lax.fori_loop(0, 2, project, tuple(jnp.zeros((8, SLOTS), F32) for _ in range(3)))
+                row = first_plane + p
+                sums[k] = sums[k] + shape_r[k, row : row + 1, :] * along[k]
+
+    project(0, 11)
+    project(11, 11)
+
     strength = charge * amplitude
     force = [jnp.sum(s, axis=0, keepdims=True) * strength for s in sums]
 
@@ -328,7 +330,7 @@
 
     for slot, device, place in plane:
         send(part.at[place], plane_in.at[slot - 1], 1, device)
-    rows = pl.ds(0, CA)
+    rows = pl.ds(8, CA)
     far = [
         send(own.at[22, rows], rad_in.at[0, 2], 2, around[0]),
         send(own.at[1, rows], rad_in.at[1, 0], 3, around[1]),
@@ -341,10 +343,9 @@
     ]
 
     def join(p):
-        value = own[p] + ax_in[p]
-        full[p] = value[0:CA]
-        edge[0, p] = value[CA : CA + 4]
-        edge[1, p] = value[CA + 4 :]
+        full[p] = own[p, 8:56] + ax_in[p, 8:56]
+        edge[0, p] = own[p, 56:60] + ax_in[p, 56:60]
+        edge[1, p] = own[p, 4:8] + ax_in[p, 4:8]
 
     ax_copies[0].wait_recv()
     join(20)
@@ -413,7 +414,7 @@
     whole = pl.BlockSpec(memory_space=pltpu.VMEM)
     operands = [start_potential, charge_density, box_anchor, box_extent, atom_center]
     operands += [atom_charge.reshape(1, ATOMS), atom_place.reshape(1, ATOMS)]
-    grid = (PLANES + 2, ROWS, CZ)
+    grid = (PLANES + 2, CA + 16, CZ)
     potential, forces = pl.pallas_call(
         kernel,
         out_shape=(

time: 30.1 us -> 29.9 us (level)
  no operation moved by 1% of the time
where the time goes in v4:
time: 29.9 us; the launch traced here: 29.7 us
  Pallas kernels  29.1 us (97%)
  between operations  0.64 us (2%)
    pallas_call x1, Pallas kernels, shards(): pl.pallas_call(kernel, out_shape=(jax.ShapeDtypeStruct((CR, CA, CZ), F32)...  28.3 us
    pallas_call x1, Pallas kernels, shards(): pl.pallas_call(store, out_shape=(jax.ShapeDtypeStruct((CR, CA, CZ), F32),...  0.77 us

profile of v4, /device:TPU:1, one launch (start us, length us, event | category | flops | bytes accessed | tf_op | source)
XLA Modules:
  0.0 29.7 jit_solution(2393463278235774679)
XLA Ops:
  0.6 28.3 %shard_map.86 = (f32[16,48,128]{2,1,0:T(8,128)S(1)}, f32[3,4]{1,0:T(4,128)S(1)}) custom-call(f32[16,48,128]{2,1,0:T(8,128)} %start_hbm.1, f32[16,48,128]{2,1,0:T(8,128)} %source_hbm.1, s32[3,2048]{1,0:T(4,128)} %anchor_hbm.1, s32[3,2048]{1,0:T(4,128)} %extent_hbm.1, f32[3,2048]{1,0:T(4,128)} %center_hbm.1, f32[1,2048]{1,0:T(1,128)} %bitcast.2, s32[1,2048]{1,0:T(1,128)} %bitcast.3), custom_call_target="tpu_custom_call" | custom-call | tf_op jit(solution)/shard_map/pallas_call | solution.py:418
  29.0 0.8 %shard_map.87 = (f32[16,48,128]{2,1,0:T(8,128)}, f32[3,4]{1,0:T(4,128)}) custom-call(f32[16,48,128]{2,1,0:T(8,128)S(1)} %get-tuple-element.4.potential_ref, f32[3,4]{1,0:T(4,128)S(1)} %get-tuple-element.5.force_ref), custom_call_target="tpu_custom_call" | custom-call | tf_op jit(solution)/shard_map/pallas_call | solution.py:453

commit v5 on v4

--- a/solution.py
+++ b/solution.py
@@ -33,10 +33,6 @@
     ]
 
 
-def far_first(count):
-    return sorted(range(1, count), key=lambda d: -min(d, count - d))
-
-
 def plane_peers(r, a, x):
     me_x, z_hi, z_lo, me_y = r // 2, lax.rem(r, 2), a // 8, lax.rem(a, 8)
     order = [(dx, dy) for dx in range(4) for dy in range(8) if dx or dy]
@@ -47,12 +43,13 @@
 
 
 def column_peers(r, a, x):
-    me_x, me_y = r // 2, lax.rem(a, 8)
-    me = (lax.rem(r, 2) * 4 + a // 8) * 2 + x
-    for d in far_first(16):
-        t = lax.rem(me + d, 16)
-        tz = t // 2
-        yield d, (me_x * 2 + tz // 4, lax.rem(tz, 4) * 8 + me_y, lax.rem(t, 2))
+    z_hi, z_lo, me_y = lax.rem(r, 2), a // 8, lax.rem(a, 8)
+    for flip in (1, 0):
+        for d in (0, 4, 3, 5, 2, 6, 1, 7):
+            if flip or d:
+                t = lax.rem(z_lo * 2 + x + d, 8)
+                half = 1 - z_hi if flip else z_hi
+                yield 8 * flip + d, ((r // 2) * 2 + half, (t // 2) * 8 + me_y, lax.rem(t, 2))
 
 
 def split2(value):
@@ -155,22 +152,10 @@
     center_ref,
     charge_ref,
     place_ref,
+    ready,
     sems,
     in_sems,
 ):
-    r, a, x = lax.axis_index("rad"), lax.axis_index("ang"), lax.axis_index("ax")
-    up, down = lax.rem(r + 1, N_RAD), lax.rem(r + N_RAD - 1, N_RAD)
-    nxt, prv = lax.rem(a + 1, N_ANG), lax.rem(a + N_ANG - 1, N_ANG)
-    plane = list(plane_peers(r, a, x))
-    column = list(column_peers(r, a, x))
-    around = [(up, a, x), (down, a, x), (r, nxt, x), (r, prv, x)]
-    around += [(up, nxt, x), (down, nxt, x), (up, prv, x), (down, prv, x)]
-
-    barrier = pltpu.get_barrier_semaphore()
-    targets = around + [p[1] for p in column] + [p[1] for p in plane]
-    for target in targets:
-        pl.semaphore_signal(barrier, inc=1, device_id=target, device_id_type=MESH)
-
     cells = (pl.ds(4, CR), pl.ds(8, CA))
     window = pl.ds(FIRST, ROWS)
     fetch = [
@@ -185,6 +170,27 @@
     fetch = [pltpu.make_async_copy(*pair, in_sems.at[k]) for k, pair in enumerate(fetch)]
     for copy in fetch:
         copy.start()
+
+    r, a, x = lax.axis_index("rad"), lax.axis_index("ang"), lax.axis_index("ax")
+    up, down = lax.rem(r + 1, N_RAD), lax.rem(r + N_RAD - 1, N_RAD)
+    nxt, prv = lax.rem(a + 1, N_ANG), lax.rem(a + N_ANG - 1, N_ANG)
+    plane = list(plane_peers(r, a, x))
+    column = list(column_peers(r, a, x))
+    around = [(up, a, x), (down, a, x), (r, nxt, x), (r, prv, x)]
+    around += [(up, nxt, x), (down, nxt, x), (up, prv, x), (down, prv, x)]
+
+    barrier = pltpu.get_barrier_semaphore()
+    far_column = [device for slot, device in column if slot >= 8]
+    targets = around + [device for slot, device in column if slot < 8] + [p[1] for p in plane]
+    odd = lax.rem(r, 2)
+    for target in targets:
+        pl.semaphore_signal(barrier, inc=1, device_id=target, device_id_type=MESH)
+
+    @pl.when(odd == 0)
+    def _():
+        for target in far_column:
+            pl.semaphore_signal(barrier, inc=1, device_id=target, device_id_type=MESH)
+
 
     strip = jnp.zeros((PLANES + 2, 8, CZ), F32)
     for ref in (va, vax, vb, vbx, src):
@@ -306,12 +312,18 @@
     here = iota((64, SLOTS), 0).astype(F32) == low
     spread = jnp.concatenate([jnp.where(here, f, 0.0) for f in force] + [jnp.zeros((64, SLOTS), F32)], axis=0)
     placed = jnp.zeros((32, 256), F32)
-    for piece in split3(spread):
-        placed = placed + nt(to, piece.astype(BF16))
+    for piece in split2(spread):
+        placed = placed + nt(to, piece)
     for k in range(32):
         part[k] = placed[k : k + 1, :]
 
-    pl.semaphore_wait(barrier, len(targets))
+    pl.semaphore_wait(barrier, len(targets) + odd * len(far_column))
+
+    @pl.when(odd == 1)
+    def _():
+        for target in far_column:
+            pl.semaphore_signal(ready, inc=1, device_id=target, device_id_type=MESH)
+
 
     def send(source, landing, number, device):
         copy = pltpu.make_async_remote_copy(
@@ -371,6 +383,11 @@
     wait(plane_in, 1, 1)
     me_place = (r // 2) * 8 + lax.rem(a, 8)
     mine[...] = part[me_place] + jnp.sum(plane_in[...], axis=0)
+
+    @pl.when(odd == 0)
+    def _():
+        pl.semaphore_wait(ready, len(far_column))
+
     for slot, device in column:
         send(mine, column_in.at[slot - 1], 10, device)
 
@@ -442,6 +459,7 @@
             pltpu.VMEM((3, ATOMS), F32),
             pltpu.VMEM((1, ATOMS), F32),
             pltpu.VMEM((1, ATOMS), jnp.int32),
+            pltpu.SemaphoreType.REGULAR,
             pltpu.SemaphoreType.DMA((2, 15)),
             pltpu.SemaphoreType.DMA((7,)),
         ],

time: 29.9 us -> 29.7 us (level)
  no operation moved by 1% of the time
where the time goes in v5:
time: 29.7 us; the launch traced here: 29.5 us
  Pallas kernels  28.9 us (97%)
  between operations  0.64 us (2%)
    pallas_call x1, Pallas kernels, shards(): pl.pallas_call(kernel, out_shape=(jax.ShapeDtypeStruct((CR, CA, CZ), F32)...  28.1 us
    pallas_call x1, Pallas kernels, shards(): pl.pallas_call(store, out_shape=(jax.ShapeDtypeStruct((CR, CA, CZ), F32),...  0.77 us

profile of v5, /device:TPU:1, one launch (start us, length us, event | category | flops | bytes accessed | tf_op | source)
XLA Modules:
  0.0 29.5 jit_solution(13807200977952074945)
XLA Ops:
  0.6 28.1 %shard_map.86 = (f32[16,48,128]{2,1,0:T(8,128)S(1)}, f32[3,4]{1,0:T(4,128)S(1)}) custom-call(f32[16,48,128]{2,1,0:T(8,128)} %start_hbm.1, f32[16,48,128]{2,1,0:T(8,128)} %source_hbm.1, s32[3,2048]{1,0:T(4,128)} %anchor_hbm.1, s32[3,2048]{1,0:T(4,128)} %extent_hbm.1, f32[3,2048]{1,0:T(4,128)} %center_hbm.1, f32[1,2048]{1,0:T(1,128)} %bitcast.2, s32[1,2048]{1,0:T(1,128)} %bitcast.3), custom_call_target="tpu_custom_call" | custom-call | tf_op jit(solution)/shard_map/pallas_call | solution.py:435
  28.7 0.8 %shard_map.87 = (f32[16,48,128]{2,1,0:T(8,128)}, f32[3,4]{1,0:T(4,128)}) custom-call(f32[16,48,128]{2,1,0:T(8,128)S(1)} %get-tuple-element.4.potential_ref, f32[3,4]{1,0:T(4,128)S(1)} %get-tuple-element.5.force_ref), custom_call_target="tpu_custom_call" | custom-call | tf_op jit(solution)/shard_map/pallas_call | solution.py:471

commit v6 on v5

--- a/solution.py
+++ b/solution.py
@@ -384,12 +384,21 @@
     me_place = (r // 2) * 8 + lax.rem(a, 8)
     mine[...] = part[me_place] + jnp.sum(plane_in[...], axis=0)
 
+    def pass_on(far):
+        for slot, device in column:
+            if (slot >= 8) == far:
+                send(mine, column_in.at[slot - 1], 10, device)
+
+    @pl.when(odd == 1)
+    def _():
+        pass_on(True)
+
+    pass_on(False)
+
     @pl.when(odd == 0)
     def _():
         pl.semaphore_wait(ready, len(far_column))
-
-    for slot, device in column:
-        send(mine, column_in.at[slot - 1], 10, device)
+        pass_on(True)
 
     for copy in copies:
         copy.wait()

time: 29.7 us -> 29.7 us (level)
  no operation moved by 1% of the time
where the time goes in v6:
time: 29.7 us; the launch traced here: 29.5 us
  Pallas kernels  28.9 us (97%)
  between operations  0.64 us (2%)
    pallas_call x1, Pallas kernels, shards(): pl.pallas_call(kernel, out_shape=(jax.ShapeDtypeStruct((CR, CA, CZ), F32)...  28.1 us
    pallas_call x1, Pallas kernels, shards(): pl.pallas_call(store, out_shape=(jax.ShapeDtypeStruct((CR, CA, CZ), F32),...  0.77 us

profile of v6, /device:TPU:1, one launch (start us, length us, event | category | flops | bytes accessed | tf_op | source)
XLA Modules:
  0.0 29.5 jit_solution(11977153784524410650)
XLA Ops:
  0.6 28.1 %shard_map.86 = (f32[16,48,128]{2,1,0:T(8,128)S(1)}, f32[3,4]{1,0:T(4,128)S(1)}) custom-call(f32[16,48,128]{2,1,0:T(8,128)} %start_hbm.1, f32[16,48,128]{2,1,0:T(8,128)} %source_hbm.1, s32[3,2048]{1,0:T(4,128)} %anchor_hbm.1, s32[3,2048]{1,0:T(4,128)} %extent_hbm.1, f32[3,2048]{1,0:T(4,128)} %center_hbm.1, f32[1,2048]{1,0:T(1,128)} %bitcast.2, s32[1,2048]{1,0:T(1,128)} %bitcast.3), custom_call_target="tpu_custom_call" | custom-call | tf_op jit(solution)/shard_map/pallas_call | solution.py:444
  28.7 0.8 %shard_map.87 = (f32[16,48,128]{2,1,0:T(8,128)}, f32[3,4]{1,0:T(4,128)}) custom-call(f32[16,48,128]{2,1,0:T(8,128)S(1)} %get-tuple-element.4.potential_ref, f32[3,4]{1,0:T(4,128)S(1)} %get-tuple-element.5.force_ref), custom_call_target="tpu_custom_call" | custom-call | tf_op jit(solution)/shard_map/pallas_call | solution.py:480
